TPU v7x, 512 devices: a whole 4x8x8 slice. The times are simulated.
512 devices in a mesh: dp: 16 (over z, x_lo), space: 32 (over x_hi, y, core).
Axes of the slice: x: 4 (x_hi: 2, x_lo: 2; x = x_hi * 2 + x_lo), y: 8, z: 8, core: 2. Of those that a mesh axis runs over, the one named last changes fastest.
Arguments:
- pre_act: bfloat16 [16, 256, 128, 320], P('dp', 'space'), may hold values from -6 to 6
- out_grad: bfloat16 [16, 256, 128, 320], P('dp', 'space'), may hold values from -6 to 6
- kernel: bfloat16 [3, 3, 320, 320], replicated, may hold values from -0.109375 to 0.109375
Outputs:
- in_grad: bfloat16 [16, 256, 128, 320], P('dp', 'space')
- kernel_grad: float32 [2880, 320], P('dp')
All inputs are finite; a program needn't handle non-finite values.
Results may differ from a plain program's by a relative error of at most 0.0029.
Values may be sent and summed in bfloat16 or wider, within the bound.
A program may use at most 64 MiB of HBM per device.

v0:
```python
import jax
import jax.numpy as jnp
from jax import lax
from jax.sharding import PartitionSpec as P


def with_halo(cells, sides, width):
    for axis, dim in sides:
        count = lax.axis_size(axis)
        ends = count - 1
        head = lax.slice_in_dim(cells, 0, width, axis=dim)
        tail = lax.slice_in_dim(cells, cells.shape[dim] - width, cells.shape[dim], axis=dim)
        cells = jnp.concatenate(
            [
                lax.ppermute(tail, axis, [(i, (i + 1) % count) for i in range(ends)]),
                cells,
                lax.ppermute(head, axis, [((i + 1) % count, i) for i in range(ends)]),
            ],
            axis=dim,
        )
    return cells


def shards(pre_act, out_grad, kernel):
    images = pre_act.shape[0]
    rows = pre_act.shape[1]
    width = pre_act.shape[2]
    chans = pre_act.shape[3]
    count_rows = images * rows * width
    pixels = count_rows * lax.axis_size("dp") * lax.axis_size("space")
    factor = float(pixels) ** (-0.5)
    stacked = jnp.stack([pre_act, out_grad])
    padded = with_halo(stacked, (("space", 2),), 1)
    padded = jnp.pad(padded, ((0, 0), (0, 0), (0, 0), (1, 1), (0, 0)))
    act_pad = jax.nn.silu(padded[0].astype(jnp.float32)).astype(jnp.bfloat16)
    grad_pad = padded[1]
    grad_taps = []
    for tap_a in range(3):
        for tap_b in range(3):
            grad_taps.append(
                grad_pad[:, 2 - tap_a : 2 - tap_a + rows, 2 - tap_b : 2 - tap_b + width, :]
            )
    grad_cols = jnp.stack(grad_taps, axis=3).reshape(count_rows, 9, chans)
    kernel_taps = kernel.reshape(9, chans, chans)
    act_grad = jnp.einsum("mtd,tcd->mc", grad_cols, kernel_taps, preferred_element_type=jnp.float32)
    pre_f = pre_act.astype(jnp.float32)
    sig = jax.nn.sigmoid(pre_f)
    deriv = sig * (1.0 + pre_f * (1.0 - sig))
    in_grad = (act_grad.reshape(images, rows, width, chans) * deriv).astype(jnp.bfloat16)
    g_flat = out_grad.reshape(count_rows, chans)
    span = 9 * chans // 9
    act_taps = []
    for tap_a in range(3):
        for tap_b in range(3):
            act_taps.append(act_pad[:, tap_a : tap_a + rows, tap_b : tap_b + width, :])
    patches = jnp.stack(act_taps, axis=3).reshape(count_rows, 9, span)
    term = jnp.einsum("mtc,md->ctd", patches, g_flat, preferred_element_type=jnp.float32)
    local_term = term.reshape(span * 9, chans) * factor
    summed = lax.psum(local_term, "space")
    kernel_grad = lax.psum_scatter(summed, "dp", scatter_dimension=0, tiled=True)
    return (in_grad, kernel_grad)


def solution(mesh):
    placed = (P("dp", "space", None, None), P("dp", "space", None, None), P())
    return jax.shard_map(
        shards,
        mesh=mesh,
        in_specs=placed,
        out_specs=(P("dp", "space", None, None), P("dp", None)),
        check_vma=False,
    )
```

profile of v0, /device:TPU:1, one launch (start us, length us, event | category | flops | bytes accessed | tf_op | source)
XLA Modules:
  0.0 479.6 jit_solution(14434711421166071963)
XLA Ops:
  7.2 1.2 pad_maximum_fusion.1
  8.4 4.6 collective-permute-start
  13.0 5.5 %collective-permute-start.1 = (bf16[2,1,1,128,320]{3,4,2,1,0:T(8,128)(2,1)S(1)}, bf16[2,1,1,128,320]{3,4,2,1,0:T(8,128)(2,1)S(1)}, u32[]{:S(2)}, u32[]{:S(2)}) collective-permute-start(bf16[2,1,1,128,320]{3,4,2,1,0:T(8,128)(2,1)S(1)} %get-tuple-element.12), channel_id=1, source_target_pairs={{1,0},{2,1},{3,2},{4,3},{5,4},{6,5},{7,6},{8,7},{9,8},{10,9},{11,1... | collective-permute-start | bytes 491528 | tf_op jit(solution)/shard_map/ppermute | solution.py:17
  18.5 1.3 dynamic-slice.4
  20.5 3.7 select_maximum_fusion
  24.2 0.9 fusion.11
  25.1 1.4 slice_bitcast_fusion.1
  27.5 0.4 fusion.35
  27.8 0.4 fusion.34
  29.1 3.3 fusion.7
  32.4 5.8 %copy.26 = f32[320,9,320]{2,1,0:T(8,128)} copy(f32[320,9,320]{2,0,1:T(8,128)S(1)} %fusion.7) | data formatting | bytes 7372800 | tf_op jit(solution)/shard_map/mul | solution.py:58
  38.2 6.8 %mul.40 = f32[2880,320]{1,0:T(8,128)} reshape(f32[320,9,320]{2,1,0:T(8,128)} %copy.26) | data formatting | bytes 7372800 | tf_op jit(solution)/shard_map/mul | solution.py:58
  45.0 104.5 %fusion = f32[192,320]{1,0:T(8,128)S(1)} fusion(f32[2880,320]{1,0:T(8,128)} %mul.40), kind=kCustom, calls=%all-reduce-scatter | all-reduce-scatter fusion | flops 983041 | bytes 3934208
  149.5 0.8 slice.108
  150.4 2.0 collective-permute-start.2
  152.4 8.8 %fusion.41 = (bf16[1,8,128,320]{2,3,1,0:T(8,128)(2,1)S(1)}, bf16[1,8,128,320]{2,3,1,0:T(8,128)(2,1)S(1)}, bf16[1,8,128,320]{2,3,1,0:T(8,128)(2,1)}, bf16[1,8,128...) fusion(bf16[1,10,130,320]{2,3,1,0:T(8,128)(2,1)} %slice_bitcast, ...), kind=kLoop, calls=%fused_computation.64 | loop fusion | bytes 11796480 | tf_op jit(solution)/shard_map/slice | solution.py:41
  161.2 1.3 copy.16
  162.4 2.1 stack.72
  164.5 2.0 constant_dynamic-update-slice_fusion.8
  166.5 2.3 copy.17
  168.9 2.1 stack.73
  171.0 2.3 copy.18
  173.3 2.1 stack.74
  175.5 2.3 copy.19
  177.8 2.2 stack.75
  180.0 2.3 copy.20
  182.3 2.2 stack.76
  184.5 2.3 copy.21
  186.9 2.1 stack.77
  189.0 2.3 copy.22
  191.3 2.1 stack.78
  193.4 1.3 copy.23
  194.7 2.2 stack.79
  196.9 1.3 copy.24
  198.1 2.1 stack.80
  200.2 2.1 constant_dynamic-update-slice_fusion.7
  202.4 2.1 constant_dynamic-update-slice_fusion.6
  204.4 0.9 constant_dynamic-update-slice_fusion.5
  205.3 2.0 constant_dynamic-update-slice_fusion.4
  207.3 2.0 constant_dynamic-update-slice_fusion.3
  209.3 0.9 constant_dynamic-update-slice_fusion.2
  210.1 0.9 constant_dynamic-update-slice_fusion.1
  211.0 0.9 constant_dynamic-update-slice_fusion
  212.0 2.1 concatenate.5
  214.1 0.7 constant_dynamic-slice_fusion
  214.9 5.9 %fusion.23 = bf16[1,8,128,320]{2,3,1,0:T(8,128)(2,1)} fusion(bf16[9,320,320,1]{2,1,0,3:T(8,128)(2,1)S(1)} %bitcast.126, bf16[1,8,128,320]{2,3,1,0:T(8,128)(2,1)S(1)} %copy-done.2, bf16[1024,9,320]{0,2,1:T(8,128)(2,1)} %constant_dynamic-update-slice_fusion), kind=kOutput, calls=%fused_computation.27 | convolution fusion | flops 1890713600 | bytes 9052160 | tf_op jit(solution)/shard_map/mtd,tcd->mc/dot_general | solution.py:45
  220.8 250.3 %all-reduce.5.cloned.1.call-done = f32[180,320]{1,0:T(8,128)} async-done(((f32[180,320]{1,0:T(8,128)}), f32[180,320]{1,0:T(8,128)}) %all-reduce.5.cloned.1.call-update) | async-done | bytes 230416 | tf_op jit(solution)/shard_map/psum | solution.py:59
  471.1 1.7 copy.57
  (28 shorter events, 2.0 us)
Async XLA Ops:
  7.2 207.7 %copy-start = (bf16[3,3,320,320]{3,2,1,0:T(8,128)(2,1)S(1)}, bf16[3,3,320,320]{3,2,1,0:T(8,128)(2,1)}, u32[]{:S(2)}) copy-start(bf16[3,3,320,320]{3,2,1,0:T(8,128)(2,1)} %param.5) | copy-start | bytes 5529604
  7.2 463.9 %all-reduce.5.cloned.1.call-start = ((), (), s32[]{:S(2)}) async-start(), calls=%async_computation | async-start | bytes 565248 | tf_op jit(solution)/shard_map/psum | solution.py:59
  8.4 12.0 %collective-permute-start = (bf16[2,1,1,128,320]{3,4,2,1,0:T(8,128)(2,1)S(1)}, bf16[2,1,1,128,320]{3,4,2,1,0:T(8,128)(2,1)S(1)}, u32[]{:S(2)}, u32[]{:S(2)}) collective-permute-start(bf16[2,1,1,128,320]{3,4,2,1,0:T(8,128)(2,1)S(1)} %get-tuple-element.11), channel_id=1, source_target_pairs={{0,1},{1,2},{2,3},{3,4},{4,5},{5,6},{6,7},{7,8},{8,9},{9,10},{10,1... | collective-permute-start | bytes 491528 | tf_op jit(solution)/shard_map/ppermute | solution.py:15
  13.0 7.4 %collective-permute-start.1 = (bf16[2,1,1,128,320]{3,4,2,1,0:T(8,128)(2,1)S(1)}, bf16[2,1,1,128,320]{3,4,2,1,0:T(8,128)(2,1)S(1)}, u32[]{:S(2)}, u32[]{:S(2)}) collective-permute-start(bf16[2,1,1,128,320]{3,4,2,1,0:T(8,128)(2,1)S(1)} %get-tuple-element.12), channel_id=1, source_target_pairs={{1,0},{2,1},{3,2},{4,3},{5,4},{6,5},{7,6},{8,7},{9,8},{10,9},{11,1... | collective-permute-start | bytes 491528 | tf_op jit(solution)/shard_map/ppermute | solution.py:17
  26.5 2.6 copy-start.1
  149.5 0.8 copy-start.7
  150.4 61.6 %collective-permute-start.2 = (f32[180,320]{1,0:T(8,128)}, f32[180,320]{1,0:T(8,128)}, u32[]{:S(2)}, u32[]{:S(2)}) collective-permute-start(f32[180,320]{1,0:T(8,128)} %slice.108), channel_id=1, source_target_pairs={{0,32},{32,64},{64,96},{96,128},{128,160},{160,192},{192,224},{224... | collective-permute-start | bytes 691208
  194.7 9.8 %copy-start.3 = (bf16[1024,1,320]{0,2,1:T(8,128)(2,1)S(1)}, bf16[1024,1,320]{0,2,1:T(8,128)(2,1)}, u32[]{:S(2)}) copy-start(bf16[1024,1,320]{0,2,1:T(8,128)(2,1)} %stack.75) | copy-start | bytes 1966084
  200.2 9.0 %copy-start.4 = (bf16[1024,1,320]{0,2,1:T(8,128)(2,1)S(1)}, bf16[1024,1,320]{0,2,1:T(8,128)(2,1)}, u32[]{:S(2)}) copy-start(bf16[1024,1,320]{0,2,1:T(8,128)(2,1)} %stack.78) | copy-start | bytes 1966084
  200.2 9.9 %copy-start.5 = (bf16[1024,1,320]{0,2,1:T(8,128)(2,1)S(1)}, bf16[1024,1,320]{0,2,1:T(8,128)(2,1)}, u32[]{:S(2)}) copy-start(bf16[1024,1,320]{0,2,1:T(8,128)(2,1)} %stack.79) | copy-start | bytes 1966084
  200.2 10.8 %copy-start.6 = (bf16[1024,1,320]{0,2,1:T(8,128)(2,1)S(1)}, bf16[1024,1,320]{0,2,1:T(8,128)(2,1)}, u32[]{:S(2)}) copy-start(bf16[1024,1,320]{0,2,1:T(8,128)(2,1)} %stack.80) | copy-start | bytes 1966084
  202.4 12.5 %copy-start.2 = (bf16[1,8,128,320]{2,3,1,0:T(8,128)(2,1)S(1)}, bf16[1,8,128,320]{2,3,1,0:T(8,128)(2,1)}, u32[]{:S(2)}) copy-start(bf16[1,8,128,320]{2,3,1,0:T(8,128)(2,1)} %param.3) | copy-start | bytes 1966084
Sparse Core Ops, SparseCore 0:
  215.0 256.0 all-reduce.4
where the time goes:
time: 482 us; the launch traced here: 480 us
  waiting for transfers between devices  250 us (52%)
  blocking collectives  105 us (22%)
  local copies, waits for them, and re-layouts  82.7 us (17%)
  between operations  14.9 us (3%)
  starting transfers between devices  12.1 us (3%)
  matrix products  9.18 us (2%)
  other arithmetic  5.82 us (1%)
    psum x1, waiting for transfers between devices, shards(): summed = lax.psum(local_term, 'space')  250 us
    unnamed x1, blocking collectives  105 us
    slice x10, local copies, waits for them, and re-layouts, shards(): grad_pad[:, 2 - tap_a:2 - tap_a + rows, 2 - tap_b:2 - tap_b + width, :]  26.7 us
    unnamed x37, local copies, waits for them, and re-layouts  21.6 us
    another operation x10, local copies, waits for them, and re-layouts, shards(): grad_cols = jnp.stack(grad_taps, axis=3).reshape(count_rows, 9, chans)  20.1 us
    mul x2, local copies, waits for them, and re-layouts, shards(): local_term = term.reshape(span * 9, chans) * factor  12.6 us
  transfers between devices with their start and end apart: 4, of which 1 were waited for; matrix products, arithmetic and copies ran while one was open for 14% of the time, Pallas kernels for 0%

commit v1 on v0

v1 whole, which is shorter than its diff:
```python
import functools

import jax
import jax.numpy as jnp
from jax import lax
from jax.experimental import pallas as pl
from jax.experimental.pallas import tpu as pltpu
from jax.sharding import PartitionSpec as P

MESH = pl.DeviceIdType.MESH
F32 = jnp.float32
BF16 = jnp.bfloat16

NX, NY, NZ = 4, 8, 8
ROWS, C, W = 8, 320, 128
BLK = 20
PARTS = ((1, "z"), (0, "x"), (2, "x"))


def nearest_last(n):
    steps = []
    for k in range(n // 2, 0, -1):
        steps.append(k)
        if n - k != k:
            steps.append(n - k)
    return steps


def kernel(
    scale, pre_hbm, og_hbm, k_hbm, in_hbm, kg_hbm,
    pre_v, og_v, k_v, in_v, act2, og2, tap_sum, part_sum,
    snd0, rcv0, snd_x, rcv_x, snd_z, rcv_z,
    sndx2, rcvx2, sndz2, rcvz2, ybuf, fin,
    load_sem, store_sem, halo_s, halo_r, c_s, c_r, x_s, x_r, z_s, z_r,
    x2_s, x2_r, z2_s, z2_r, y_s, y_r, f_s, f_r,
):
    dp = lax.axis_index("dp")
    sp = lax.axis_index("space")
    z = dp // 2
    xlo = lax.rem(dp, 2)
    core = lax.rem(sp, 2)
    y = lax.rem(sp // 2, NY)
    xhi = sp // (2 * NY)
    x = xhi * 2 + xlo

    def dev(z_, x_, y_, core_):
        return {"dp": z_ * 2 + lax.rem(x_, 2), "space": ((x_ // 2) * NY + y_) * 2 + core_}

    def xp(k):
        return lax.rem(x + k, NX)

    def yp(k):
        return lax.rem(y + k, NY)

    def zp(k):
        return lax.rem(z + k, NZ)

    up = {"dp": dp, "space": lax.rem(sp + 31, 32)}
    down = {"dp": dp, "space": lax.rem(sp + 1, 32)}
    mate = dev(z, x, y, 1 - core)
    far = dev(z, xp(2), y, core)
    far_mate = dev(z, xp(2), y, 1 - core)

    loads = [
        pltpu.make_async_copy(og_hbm, og_v.at[pl.ds(1, ROWS)], load_sem.at[0]),
        pltpu.make_async_copy(pre_hbm, pre_v, load_sem.at[1]),
        pltpu.make_async_copy(k_hbm, k_v, load_sem.at[2]),
    ]
    for c in loads:
        c.start()

    barrier = pltpu.get_barrier_semaphore()
    greeted = [up, down, far_mate]
    greeted += [dev(z, xp(k), y, core) for k in range(1, NX)]
    greeted += [dev(z, x, yp(k), core) for k in range(1, NY)]
    greeted += [dev(zp(k), x, y, core) for k in range(1, NZ)]
    for d in greeted:
        pl.semaphore_signal(barrier, inc=1, device_id=d, device_id_type=MESH)

    def shifts(r, value):
        lanes = pl.ds(r * W, W)
        og2[1, :, lanes] = value
        wide = value.astype(F32)
        col = lax.broadcasted_iota(jnp.int32, (C, W), 1)
        og2[0, :, lanes] = jnp.where(col == W - 1, 0.0, pltpu.roll(wide, W - 1, 1)).astype(BF16)
        og2[2, :, lanes] = jnp.where(col == 0, 0.0, pltpu.roll(wide, 1, 1)).astype(BF16)

    loads[0].wait()
    for r in range(1, ROWS + 1):
        shifts(r, og_v[r])
    loads[1].wait()
    for r in range(ROWS):
        v = pre_v[r].astype(F32)
        act2[:, pl.ds(r * W, W)] = (v * (1.0 / (1.0 + jnp.exp(-v)))).astype(BF16)

    pl.semaphore_wait(barrier, len(greeted))

    halos = [
        pltpu.make_async_remote_copy(
            src_ref=og_hbm.at[ROWS - 1], dst_ref=og_v.at[0], send_sem=halo_s.at[0], recv_sem=halo_r.at[0],
            device_id=down, device_id_type=MESH),
        pltpu.make_async_remote_copy(
            src_ref=og_hbm.at[0], dst_ref=og_v.at[ROWS + 1], send_sem=halo_s.at[1], recv_sem=halo_r.at[1],
            device_id=up, device_id_type=MESH),
    ]
    for c in halos:
        c.start()

    def tap_row(p, a):
        for b in range(3):
            tap_sum[b] = lax.dot_general(
                act2[...], og2[b, :, pl.ds((2 - a) * W, ROWS * W)],
                (((1,), (1,)), ((), ())), preferred_element_type=F32)
        for blk in range(16):
            for b in range(3):
                part_sum[p, blk // 2, blk % 2, pl.ds(b * BLK, BLK), :] = tap_sum[b, pl.ds(blk * BLK, BLK), :]
            part_sum[p, blk // 2, blk % 2, pl.ds(3 * BLK, 4), :] = jnp.zeros((4, C), F32)

    def core_copy(p):
        return pltpu.make_async_remote_copy(
            src_ref=snd0.at[p], dst_ref=rcv0.at[p], send_sem=c_s.at[p], recv_sem=c_r.at[p],
            device_id=mate, device_id_type=MESH)

    def core_send(p):
        for zb in range(NZ):
            for xl in range(2):
                for half in range(2):
                    rows = pl.ds(pl.multiple_of((1 - core) * 32 + half * 16, 16), 16)
                    snd0[p, zb, xl, half] = part_sum[p, zb, xl, rows, :].astype(BF16)
        core_copy(p).start()

    def chip_rows(p, zb, xl, half):
        mine = part_sum[p, zb, xl, pl.ds(pl.multiple_of(core * 32 + half * 16, 16), 16), :]
        return mine + rcv0[p, zb, xl, half].astype(F32)

    def first_copy(p, i, k):
        if PARTS[p][1] == "x":
            q = p - 1
            peer = xp(k)
            return pltpu.make_async_remote_copy(
                src_ref=snd_x.at[q, peer], dst_ref=rcv_x.at[q, x], send_sem=x_s.at[q, i], recv_sem=x_r.at[q, x],
                device_id=dev(z, peer, y, core), device_id_type=MESH), peer
        peer = zp(k)
        return pltpu.make_async_remote_copy(
            src_ref=snd_z.at[peer], dst_ref=rcv_z.at[z], send_sem=z_s.at[i], recv_sem=z_r.at[z],
            device_id=dev(peer, x, y, core), device_id_type=MESH), peer

    def first_recv(p, peer):
        if PARTS[p][1] == "x":
            q = p - 1
            return pltpu.make_async_remote_copy(
                src_ref=snd_x.at[q, peer], dst_ref=rcv_x.at[q, peer], send_sem=x_s.at[q, 0], recv_sem=x_r.at[q, peer],
                device_id=mate, device_id_type=MESH)
        return pltpu.make_async_remote_copy(
            src_ref=snd_z.at[peer], dst_ref=rcv_z.at[peer], send_sem=z_s.at[0], recv_sem=z_r.at[peer],
            device_id=mate, device_id_type=MESH)

    def first_steps(p):
        return nearest_last(NX if PARTS[p][1] == "x" else NZ)

    def first_send(p):
        core_copy(p).wait_recv()
        if PARTS[p][1] == "x":
            for zb in range(NZ):
                for xx in range(NX):
                    snd_x[p - 1, xx, zb] = chip_rows(p, zb, xx % 2, xx // 2).astype(BF16)
        else:
            for zb in range(NZ):
                for xx in range(NX):
                    snd_z[zb, xx] = chip_rows(p, zb, xx % 2, xx // 2).astype(BF16)
        for i, k in enumerate(first_steps(p)):
            first_copy(p, i, k)[0].start()

    def second_copy(p, i, k):
        if PARTS[p][1] == "x":
            q = p - 1
            peer = zp(k)
            return pltpu.make_async_remote_copy(
                src_ref=sndz2.at[q, peer], dst_ref=rcvz2.at[q, z], send_sem=z2_s.at[q, i], recv_sem=z2_r.at[q, z],
                device_id=dev(peer, x, y, core), device_id_type=MESH), peer
        peer = xp(k)
        return pltpu.make_async_remote_copy(
            src_ref=sndx2.at[peer], dst_ref=rcvx2.at[x], send_sem=x2_s.at[i], recv_sem=x2_r.at[x],
            device_id=dev(z, peer, y, core), device_id_type=MESH), peer

    def second_recv(p, peer):
        if PARTS[p][1] == "x":
            q = p - 1
            return pltpu.make_async_remote_copy(
                src_ref=sndz2.at[q, peer], dst_ref=rcvz2.at[q, peer], send_sem=z2_s.at[q, 0], recv_sem=z2_r.at[q, peer],
                device_id=mate, device_id_type=MESH)
        return pltpu.make_async_remote_copy(
            src_ref=sndx2.at[peer], dst_ref=rcvx2.at[peer], send_sem=x2_s.at[0], recv_sem=x2_r.at[peer],
            device_id=mate, device_id_type=MESH)

    def second_steps(p):
        return nearest_last(NZ if PARTS[p][1] == "x" else NX)

    def second_send(p):
        for k in first_steps(p):
            peer = xp(k) if PARTS[p][1] == "x" else zp(k)
            first_recv(p, peer).wait_recv()
        if PARTS[p][1] == "x":
            q = p - 1
            for zb in range(NZ):
                total = chip_rows(p, zb, xlo, xhi)
                for k in range(1, NX):
                    total = total + rcv_x[q, xp(k), zb].astype(F32)
                sndz2[q, zb] = total
        else:
            for xx in range(NX):
                total = chip_rows(p, z, xx % 2, xx // 2)
                for k in range(1, NZ):
                    total = total + rcv_z[zp(k), xx].astype(F32)
                sndx2[xx] = total
        for i, k in enumerate(second_steps(p)):
            second_copy(p, i, k)[0].start()

    def y_copy(p, i, k):
        peer = yp(k)
        return pltpu.make_async_remote_copy(
            src_ref=ybuf.at[p, y], dst_ref=ybuf.at[p, y], send_sem=y_s.at[p, i], recv_sem=y_r.at[p, y],
            device_id=dev(z, x, peer, core), device_id_type=MESH)

    def y_recv(p, peer):
        return pltpu.make_async_remote_copy(
            src_ref=ybuf.at[p, peer], dst_ref=ybuf.at[p, peer], send_sem=y_s.at[p, 0], recv_sem=y_r.at[p, peer],
            device_id=mate, device_id_type=MESH)

    def y_send(p):
        for k in second_steps(p):
            peer = zp(k) if PARTS[p][1] == "x" else xp(k)
            second_recv(p, peer).wait_recv()
        if PARTS[p][1] == "x":
            q = p - 1
            total = sndz2[q, z]
            for k in range(1, NZ):
                total = total + rcvz2[q, zp(k)]
        else:
            total = sndx2[x]
            for k in range(1, NX):
                total = total + rcvx2[xp(k)]
        ybuf[p, y] = (total * scale).astype(BF16)
        for i, k in enumerate(nearest_last(NY)):
            y_copy(p, i, k).start()

    def f_copies(p):
        slot = fin.at[p, core, xhi]
        return [
            pltpu.make_async_remote_copy(
                src_ref=slot, dst_ref=slot, send_sem=f_s.at[p, i], recv_sem=f_r.at[p, i],
                device_id=d, device_id_type=MESH)
            for i, d in enumerate((far_mate, far, mate))
        ]

    def f_recvs(p):
        slots = ((1 - core, 1 - xhi), (core, 1 - xhi), (1 - core, xhi))
        return [
            pltpu.make_async_remote_copy(
                src_ref=fin.at[p, cc, hh], dst_ref=fin.at[p, cc, hh], send_sem=f_s.at[p, i], recv_sem=f_r.at[p, i],
                device_id=mate, device_id_type=MESH)
            for i, (cc, hh) in enumerate(slots)
        ]

    def f_send(p):
        for k in nearest_last(NY):
            y_recv(p, yp(k)).wait_recv()
        total = ybuf[p, 0].astype(F32)
        for yy in range(1, NY):
            total = total + ybuf[p, yy].astype(F32)
        fin[p, core, xhi] = total
        for c in f_copies(p):
            c.start()

    def in_grad(pair):
        lanes = pair * 2 * W
        total = jnp.zeros((C, 2 * W), F32)
        for a in range(3):
            for b in range(3):
                total = total + jnp.dot(
                    k_v[a, b], og2[b, :, pl.ds((2 - a) * W + lanes, 2 * W)], preferred_element_type=F32)
        for i in range(2):
            v = pre_v[pair * 2 + i].astype(F32)
            s = 1.0 / (1.0 + jnp.exp(-v))
            in_v[pair * 2 + i] = (total[:, i * W : (i + 1) * W] * (s * (1.0 + v * (1.0 - s)))).astype(BF16)

    tap_row(0, PARTS[0][0])
    core_send(0)
    for i, (c, edge) in enumerate(zip(halos, (sp == 0, sp == 31))):
        c.wait_recv()
        r = i * (ROWS + 1)
        shifts(r, jnp.where(edge, jnp.zeros((C, W), BF16), og_v[r]))
    first_send(0)
    tap_row(1, PARTS[1][0])
    core_send(1)
    tap_row(2, PARTS[2][0])
    first_send(1)
    core_send(2)
    loads[2].wait()
    in_grad(0)
    first_send(2)
    in_grad(1)
    in_grad(2)
    second_send(1)
    in_grad(3)
    in_store = pltpu.make_async_copy(in_v, in_hbm, store_sem.at[0])
    in_store.start()
    second_send(0)
    second_send(2)
    y_send(0)
    y_send(1)
    y_send(2)
    for p in range(3):
        f_send(p)
    stores = []
    for p in range(3):
        for c in f_recvs(p):
            c.wait_recv()
        c = pltpu.make_async_copy(fin.at[p], kg_hbm.at[PARTS[p][0]], store_sem.at[1 + p])
        c.start()
        stores.append(c)

    for c in halos:
        c.wait_send()
    for p in range(3):
        core_copy(p).wait_send()
        for i, k in enumerate(first_steps(p)):
            first_copy(p, i, k)[0].wait_send()
        for i, k in enumerate(second_steps(p)):
            second_copy(p, i, k)[0].wait_send()
        for i, k in enumerate(nearest_last(NY)):
            y_copy(p, i, k).wait_send()
        for c in f_copies(p):
            c.wait_send()
    in_store.wait()
    for c in stores:
        c.wait()


def shards(scale, pre_act, out_grad, weights):
    to_rows = lambda t: jnp.swapaxes(t[0], 1, 2)
    vm, sem = pltpu.VMEM, pltpu.SemaphoreType.DMA
    grad, sums = pl.pallas_call(
        functools.partial(kernel, scale),
        out_shape=(
            jax.ShapeDtypeStruct((ROWS, C, W), BF16),
            jax.ShapeDtypeStruct((3, 2, 2, 16, C), F32),
        ),
        in_specs=[pl.BlockSpec(memory_space=pl.ANY)] * 3,
        out_specs=(pl.BlockSpec(memory_space=pl.ANY),) * 2,
        scratch_shapes=[
            vm((ROWS, C, W), BF16),
            vm((ROWS + 2, C, W), BF16),
            vm((3, 3, C, C), BF16),
            vm((ROWS, C, W), BF16),
            vm((C, ROWS * W), BF16),
            vm((3, C, (ROWS + 2) * W), BF16),
            vm((3, C, C), F32),
            vm((3, NZ, 2, 64, C), F32),
            vm((3, NZ, 2, 2, 16, C), BF16),
            vm((3, NZ, 2, 2, 16, C), BF16),
            vm((2, NX, NZ, 16, C), BF16),
            vm((2, NX, NZ, 16, C), BF16),
            vm((NZ, NX, 16, C), BF16),
            vm((NZ, NX, 16, C), BF16),
            vm((NX, 16, C), F32),
            vm((NX, 16, C), F32),
            vm((2, NZ, 16, C), F32),
            vm((2, NZ, 16, C), F32),
            vm((3, NY, 16, C), BF16),
            vm((3, 2, 2, 16, C), F32),
            sem((3,)), sem((4,)), sem((2,)), sem((2,)), sem((3,)), sem((3,)),
            sem((2, 3)), sem((2, NX)), sem((7,)), sem((NZ,)),
            sem((3,)), sem((NX,)), sem((2, 7)), sem((2, NZ)),
            sem((3, 7)), sem((3, NY)), sem((3, 3)), sem((3, 3)),
        ],
        compiler_params=pltpu.CompilerParams(collective_id=0, has_side_effects=True),
    )(to_rows(pre_act), to_rows(out_grad), weights)
    in_grad = jnp.swapaxes(grad, 1, 2)[None]
    sums = sums.reshape(3, 64, C)[:, : 3 * BLK].reshape(9, BLK, C)
    return in_grad, jnp.swapaxes(sums, 0, 1).reshape(9 * BLK, C)


def solution(mesh):
    placed = P("dp", "space", None, None)

    def whole(pre_act, out_grad, weights):
        pixels = pre_act.shape[0] * pre_act.shape[1] * pre_act.shape[2]
        return jax.shard_map(
            functools.partial(shards, float(pixels) ** -0.5),
            mesh=mesh,
            in_specs=(placed, placed, P()),
            out_specs=(placed, P("dp", None)),
            check_vma=False,
        )(pre_act, out_grad, weights)

    return whole
```

time: 482 us -> 53.8 us (0.11)
  waiting for transfers between devices: 250 us -> 0 us
  blocking collectives: 105 us -> 0 us
  local copies, waits for them, and re-layouts: 82.7 us -> 2.73 us
  Pallas kernels: 0 us -> 50.1 us
  between operations: 14.9 us -> 0.66 us
  starting transfers between devices: 12.1 us -> 0 us
  matrix products: 9.18 us -> 0 us
  other arithmetic: 5.82 us -> 0 us
    psum x1 -> x0, waiting for transfers between devices: 250 us -> none  [shards(): summed = lax.psum(local_term, 'space')]
    unnamed x1 -> x0, blocking collectives: 105 us -> none
    pallas_call x0 -> x1, Pallas kernels: none -> 50.1 us  [shards(): pl.pallas_call(functools.partial(kernel, scale), out_shape=(jax.ShapeDtyp...]
    slice x10 -> x0, local copies, waits for them, and re-layouts: 26.7 us -> none  [shards(): grad_pad[:, 2 - tap_a:2 - tap_a + rows, 2 - tap_b:2 - tap_b + width, :]]
    unnamed x37 -> x3, local copies, waits for them, and re-layouts: 21.6 us -> 0.84 us
    another operation x11 -> x0, local copies, waits for them, and re-layouts: 20.5 us -> none  [the longest x10 20.1 us: shards(): grad_cols = jnp.stack(grad_taps, axis=3).reshape(count_rows, 9, chans)]
    mul x2 -> x0, local copies, waits for them, and re-layouts: 12.6 us -> none  [shards(): local_term = term.reshape(span * 9, chans) * factor]
    ppermute x2 -> x0, starting transfers between devices: 10.1 us -> none  [the longest x1 5.49 us: with_halo(): lax.ppermute(head, axis, [((i + 1) % count, i) for i in range(ends)])]
  transfers between devices with their start and end apart: 4 -> 0, of which waited for: 1 -> 0; matrix products, arithmetic and copies ran while one was open for 14% -> 0% of each run, Pallas kernels for 0% -> 0%
where the time goes in v1:
time: 53.8 us; the launch traced here: 53.5 us
  Pallas kernels  50.1 us (93%)
  local copies, waits for them, and re-layouts  2.73 us (5%)
  between operations  0.66 us (1%)
    pallas_call x1, Pallas kernels, shards(): pl.pallas_call(functools.partial(kernel, scale), out_shape=(jax.ShapeDtyp...  50.1 us

profile of v1, /device:TPU:1, one launch (start us, length us, event | category | flops | bytes accessed | tf_op | source)
XLA Modules:
  0.0 53.5 jit_solution(6192999014388300208)
XLA Ops:
  0.6 50.1 %shard_map.50 = (bf16[8,320,128]{2,1,0:T(8,128)(2,1)}, f32[3,2,2,16,320]{4,3,2,1,0:T(8,128)}) custom-call(bf16[8,320,128]{2,1,0:T(8,128)(2,1)} %bitcast.13, bf16[8,320,128]{2,1,0:T(8,128)(2,1)} %bitcast.14, bf16[3,3,320,320]{3,2,1,0:T(8,128)(2,1)} %k_hbm.1), custom_call_target="tpu_custom_call" | custom-call | tf_op jit(solution)/shard_map/pallas_call | solution.py:343
  50.8 0.0 copy-start
  50.8 1.1 %reshape.14 = f32[9,20,320]{2,1,0:T(8,128)S(1)} reshape(f32[3,60,320]{2,1,0:T(8,128)} %bitcast.16) | data formatting | bytes 460800 | tf_op jit(solution)/shard_map/reshape | solution.py:380
  51.8 0.1 copy.6
  51.9 0.8 %reshape.15 = f32[180,320]{1,0:T(8,128)} reshape(f32[20,9,320]{2,1,0:T(8,128)S(1)} %copy.6) | data formatting | bytes 460800 | tf_op jit(solution)/shard_map/reshape | solution.py:381
  52.7 0.0 copy-done
  52.7 0.8 %copy.8 = bf16[1,8,128,320]{2,3,1,0:T(8,128)(2,1)} copy(bf16[1,8,128,320]{2,3,1,0:T(8,128)(2,1)S(1)} %bitcast.15) | data formatting | bytes 1310720
Async XLA Ops:
  50.8 1.9 %copy-start = (bf16[8,320,128]{2,1,0:T(8,128)(2,1)S(1)}, bf16[8,320,128]{2,1,0:T(8,128)(2,1)}, u32[]{:S(2)}) copy-start(bf16[8,320,128]{2,1,0:T(8,128)(2,1)} %get-tuple-element.4) | copy-start | bytes 1966084

commit v2 on v0

v2 whole, which is shorter than its diff:
```python
import functools

import jax
import jax.numpy as jnp
from jax import lax
from jax.experimental import pallas as pl
from jax.experimental.pallas import tpu as pltpu
from jax.sharding import PartitionSpec as P

MESH = pl.DeviceIdType.MESH
F32 = jnp.float32
BF16 = jnp.bfloat16

NX, NY, NZ = 4, 8, 8
ROWS, C, W = 8, 320, 128
BLK = 20
ZROWS = 2 * BLK
LANES, TILES = 1024, 8
BF16, SECOND_T, BF16 = BF16, F32, BF16
PARTS = (1, 0, 2)
ZROWS = 2 * BLK
XROWS = (16, 32, 24)
LANES, TILES = 1024, 8


def nearest_last(n):
    steps = []
    for k in range(n // 2, 0, -1):
        steps.append(k)
        if n - k != k:
            steps.append(n - k)
    return steps


def kernel(
    scale, pre_hbm, og_hbm, k_hbm, in_hbm, kg_hbm,
    pre_v, og_v, k_v, in_v, kg_v, act2, og2, part_sum,
    rcv0, snd_x, rcv_x, snd_z, rcv_z,
    sndx2, rcvx2, sndz2, rcvz2, own2, ybuf, done, fin,
    load_sem, store_sem, halo_s, halo_r, c_s, c_r, x_s, x_r, z_s, z_r,
    x2_s, x2_r, z2_s, z2_r, y_s, y_r, f_s, f_r,
):
    dp = lax.axis_index("dp")
    sp = lax.axis_index("space")
    z = dp // 2
    xlo = lax.rem(dp, 2)
    core = lax.rem(sp, 2)
    y = lax.rem(sp // 2, NY)
    x = (sp // (2 * NY)) * 2 + xlo

    def dev(z_, x_, y_, core_):
        return {"dp": z_ * 2 + lax.rem(x_, 2), "space": ((x_ // 2) * NY + y_) * 2 + core_}

    def xp(k):
        return lax.rem(x + k, NX)

    def yp(k):
        return lax.rem(y + k, NY)

    def zp(k):
        return lax.rem(z + k, NZ)

    up = {"dp": dp, "space": lax.rem(sp + 31, 32)}
    down = {"dp": dp, "space": lax.rem(sp + 1, 32)}
    mate = dev(z, x, y, 1 - core)

    barrier = pltpu.get_barrier_semaphore()
    greeted = [dev(zp(k), x, y, core) for k in nearest_last(NZ)]
    greeted += [dev(z, x, yp(k), core) for k in nearest_last(NY)]
    greeted += [dev(z, xp(k), y, core) for k in nearest_last(NX)]
    greeted += [dev(z, xp(k), y, 1 - core) for k in nearest_last(NX)]
    greeted += [up, down]
    for d in greeted:
        pl.semaphore_signal(barrier, inc=1, device_id=d, device_id_type=MESH)

    loads = [
        pltpu.make_async_copy(og_hbm, og_v.at[pl.ds(1, ROWS)], load_sem.at[0]),
        pltpu.make_async_copy(pre_hbm, pre_v, load_sem.at[1]),
        pltpu.make_async_copy(k_hbm, k_v, load_sem.at[2]),
    ]
    loads[0].start()
    loads[1].start()
    og2[pl.ds(3 * C, LANES - 3 * C), :] = jnp.zeros((LANES - 3 * C, (ROWS + 2) * W), BF16)

    def shifts(r, value):
        lanes = pl.ds(r * W, W)
        og2[pl.ds(C, C), lanes] = value
        wide = value.astype(F32)
        col = lax.broadcasted_iota(jnp.int32, (C, W), 1)
        og2[pl.ds(0, C), lanes] = jnp.where(col == W - 1, 0.0, pltpu.roll(wide, W - 1, 1)).astype(BF16)
        og2[pl.ds(2 * C, C), lanes] = jnp.where(col == 0, 0.0, pltpu.roll(wide, 1, 1)).astype(BF16)

    def tap_row(p):
        a = PARTS[p]
        total = lax.dot_general(
            act2[...], og2[:, pl.ds((2 - a) * W, ROWS * W)], (((1,), (1,)), ((), ())), preferred_element_type=F32)
        for t in range(TILES):
            part_sum[p, t] = total[:, t * W : (t + 1) * W]

    def core_copy(p):
        return pltpu.make_async_remote_copy(
            src_ref=part_sum.at[p, pl.ds((1 - core) * NX, NX)], dst_ref=rcv0.at[p], send_sem=c_s.at[p], recv_sem=c_r.at[p],
            device_id=mate, device_id_type=MESH)

    def core_send(p):
        core_copy(p).start()

    def x_slot(ref, p, peer):
        return ref.at[p, peer, :, pl.ds(0, XROWS[p])]

    def z_slot(ref, p, peer):
        return ref.at[p, peer, :, pl.ds(0, ZROWS - XROWS[p])]

    def x2_slot(ref, p, peer):
        return ref.at[p, peer, pl.ds(0, ZROWS - XROWS[p])]

    def z2_slot(ref, p, peer):
        return ref.at[p, peer, pl.ds(0, XROWS[p])]

    def x_copy(p, i, k):
        return pltpu.make_async_remote_copy(
            src_ref=x_slot(snd_x, p, xp(k)), dst_ref=x_slot(rcv_x, p, x), send_sem=x_s.at[p, i], recv_sem=x_r.at[p, x],
            device_id=dev(z, xp(k), y, core), device_id_type=MESH)

    def z_copy(p, i, k):
        return pltpu.make_async_remote_copy(
            src_ref=z_slot(snd_z, p, zp(k)), dst_ref=z_slot(rcv_z, p, z), send_sem=z_s.at[p, i], recv_sem=z_r.at[p, z],
            device_id=dev(zp(k), x, y, core), device_id_type=MESH)

    def x2_copy(p, i, k):
        return pltpu.make_async_remote_copy(
            src_ref=x2_slot(sndx2, p, xp(k)), dst_ref=x2_slot(rcvx2, p, x), send_sem=x2_s.at[p, i], recv_sem=x2_r.at[p, x],
            device_id=dev(z, xp(k), y, core), device_id_type=MESH)

    def z2_copy(p, i, k):
        return pltpu.make_async_remote_copy(
            src_ref=z2_slot(sndz2, p, zp(k)), dst_ref=z2_slot(rcvz2, p, z), send_sem=z2_s.at[p, i], recv_sem=z2_r.at[p, z],
            device_id=dev(zp(k), x, y, core), device_id_type=MESH)

    def arrived(slot, snd, rcv, s_sem, r_sem, p, peer):
        pltpu.make_async_remote_copy(
            src_ref=slot(snd, p, peer), dst_ref=slot(rcv, p, peer), send_sem=s_sem.at[p, 0], recv_sem=r_sem.at[p, peer],
            device_id=mate, device_id_type=MESH).wait_recv()

    def first_send(p):
        core_copy(p).wait_recv()
        for i, k in enumerate(nearest_last(NZ)):
            snd_z[p, zp(k), :, : ZROWS - XROWS[p]] = z_own(p, zp(k)).astype(BF16)
            z_copy(p, i, k).start()
        for i, k in enumerate(nearest_last(NX)):
            snd_x[p, xp(k), :, : XROWS[p]] = x_own(p, xp(k)).astype(BF16)
            x_copy(p, i, k).start()

    def x_own(p, t):
        total = part_sum[p, core * NX + t] + rcv0[p, t]
        return total.reshape(NZ, ZROWS, W)[:, : XROWS[p]]

    def z_own(p, zb):
        rows = pl.ds(pl.multiple_of(zb * ZROWS + XROWS[p], 8), ZROWS - XROWS[p])
        return jnp.stack([
            part_sum[p, core * NX + t, rows, :] + rcv0[p, t, rows, :] for t in range(NX)])

    def x_done(p):
        for k in nearest_last(NX):
            arrived(x_slot, snd_x, rcv_x, x_s, x_r, p, xp(k))
        total = x_own(p, x)
        for k in range(1, NX):
            total = total + rcv_x[p, xp(k), :, : XROWS[p]].astype(F32)
        sndz2[p, :, : XROWS[p]] = total.astype(BF16)
        own2[p, :, : XROWS[p]] = total
        for i, k in enumerate(nearest_last(NZ)):
            z2_copy(p, i, k).start()

    def z_done(p):
        for k in nearest_last(NZ):
            arrived(z_slot, snd_z, rcv_z, z_s, z_r, p, zp(k))
        total = z_own(p, z)
        for k in range(1, NZ):
            total = total + rcv_z[p, zp(k), :, : ZROWS - XROWS[p]].astype(F32)
        sndx2[p, :, : ZROWS - XROWS[p]] = total
        for i, k in enumerate(nearest_last(NX)):
            x2_copy(p, i, k).start()

    def y_copy(p, i, k):
        peer = yp(k)
        return pltpu.make_async_remote_copy(
            src_ref=ybuf.at[p, y], dst_ref=ybuf.at[p, y], send_sem=y_s.at[p, i], recv_sem=y_r.at[p, y],
            device_id=dev(z, x, peer, core), device_id_type=MESH)

    def y_recv(p, k):
        peer = yp(k)
        return pltpu.make_async_remote_copy(
            src_ref=ybuf.at[p, peer], dst_ref=ybuf.at[p, peer], send_sem=y_s.at[p, 0], recv_sem=y_r.at[p, peer],
            device_id=mate, device_id_type=MESH)

    def y_send(p):
        for k in nearest_last(NZ):
            arrived(z2_slot, sndz2, rcvz2, z2_s, z2_r, p, zp(k))
        upper = own2[p, z, : XROWS[p]]
        for k in range(1, NZ):
            upper = upper + rcvz2[p, zp(k), : XROWS[p]].astype(F32)
        for k in nearest_last(NX):
            arrived(x2_slot, sndx2, rcvx2, x2_s, x2_r, p, xp(k))
        lower = sndx2[p, x, : ZROWS - XROWS[p]]
        for k in range(1, NX):
            lower = lower + rcvx2[p, xp(k), : ZROWS - XROWS[p]]
        total = jnp.concatenate([upper, lower], axis=0)
        ybuf[p, y] = (total * scale).astype(BF16)
        for i, k in enumerate(nearest_last(NY)):
            y_copy(p, i, k).start()

    ENDS = [(k, other) for k in (2, 1, 3, 0) for other in (1, 0) if (k, other) != (0, 0)]

    def end_rows(xx):
        return pl.ds(pl.multiple_of(lax.rem(xx, 2) * 16, 8), 24)

    def f_copy(p, i, k, other):
        return pltpu.make_async_remote_copy(
            src_ref=done.at[p, end_rows(xp(k))], dst_ref=fin.at[p, core * NX + x],
            send_sem=f_s.at[p, i], recv_sem=f_r.at[p, core * NX + x],
            device_id=dev(z, xp(k), y, 1 - core if other else core), device_id_type=MESH)

    def f_recv(p, k, other):
        tile = (1 - core if other else core) * NX + xp(k)
        return pltpu.make_async_remote_copy(
            src_ref=done.at[p, end_rows(x)], dst_ref=fin.at[p, tile],
            send_sem=f_s.at[p, 0], recv_sem=f_r.at[p, tile], device_id=mate, device_id_type=MESH)

    def f_send(p):
        for k in nearest_last(NY):
            y_recv(p, k).wait_recv()
        total = ybuf[p, 0].astype(F32)
        for yy in range(1, NY):
            total = total + ybuf[p, yy].astype(F32)
        done[p] = total
        for i, (k, other) in enumerate(ENDS):
            f_copy(p, i, k, other).start()
        fin[p, core * NX + x] = done[p, end_rows(x), :]

    def finish(p):
        for k, other in ENDS:
            f_recv(p, k, other).wait_recv()
        wide = jnp.concatenate([fin[p, t] for t in range(TILES)], axis=1)
        wide = jnp.where(xlo == 0, wide[:BLK], wide[4 : 4 + BLK])
        for b in range(3):
            tap = wide[:, b * C : b * C + 3 * W]
            for t in range(3):
                kg_v[t, pl.ds(PARTS[p] * 3 + b, BLK, stride=9), :] = tap[:, t * W : (t + 1) * W]

    def in_grad(pair):
        lanes = pair * 2 * W
        total = jnp.zeros((C, 2 * W), F32)
        for a in range(3):
            for b in range(3):
                total = total + jnp.dot(
                    k_v[a, b], og2[pl.ds(b * C, C), pl.ds((2 - a) * W + lanes, 2 * W)], preferred_element_type=F32)
        for i in range(2):
            v = pre_v[pair * 2 + i].astype(F32)
            s = 1.0 / (1.0 + jnp.exp(-v))
            in_v[pair * 2 + i] = (total[:, i * W : (i + 1) * W] * (s * (1.0 + v * (1.0 - s)))).astype(BF16)

    halos = [
        pltpu.make_async_remote_copy(
            src_ref=og_hbm.at[ROWS - 1], dst_ref=og_v.at[0], send_sem=halo_s.at[0], recv_sem=halo_r.at[0],
            device_id=down, device_id_type=MESH),
        pltpu.make_async_remote_copy(
            src_ref=og_hbm.at[0], dst_ref=og_v.at[ROWS + 1], send_sem=halo_s.at[1], recv_sem=halo_r.at[1],
            device_id=up, device_id_type=MESH),
    ]

    loads[0].wait()
    for r in range(1, ROWS + 1):
        shifts(r, og_v[r])
    loads[1].wait()
    loads[2].start()
    for r in range(ROWS):
        v = pre_v[r].astype(F32)
        act2[:, pl.ds(r * W, W)] = (v * (1.0 / (1.0 + jnp.exp(-v)))).astype(BF16)
    tap_row(0)
    pl.semaphore_wait(barrier, len(greeted))
    for c in halos:
        c.start()
    core_send(0)
    first_send(0)
    for i, (c, edge) in enumerate(zip(halos, (sp == 0, sp == 31))):
        c.wait_recv()
        r = i * (ROWS + 1)
        shifts(r, jnp.where(edge, jnp.zeros((C, W), BF16), og_v[r]))
    tap_row(1)
    core_send(1)
    tap_row(2)
    core_send(2)
    first_send(1)
    first_send(2)
    loads[2].wait()
    for q in range(4):
        in_grad(q)
    in_store = pltpu.make_async_copy(in_v, in_hbm, store_sem.at[0])
    in_store.start()
    x_done(0)
    z_done(0)
    x_done(1)
    x_done(2)
    z_done(1)
    z_done(2)
    for p in range(3):
        y_send(p)
    for p in range(3):
        f_send(p)
    for p in range(3):
        finish(p)
    kg_stores = [
        pltpu.make_async_copy(kg_v.at[t], kg_hbm.at[:, pl.ds(t * W, W)], store_sem.at[1 + t]) for t in range(3)
    ]
    for c in kg_stores:
        c.start()

    for c in halos:
        c.wait_send()
    for p in range(3):
        core_copy(p).wait_send()
        for i, k in enumerate(nearest_last(NX)):
            x_copy(p, i, k).wait_send()
            x2_copy(p, i, k).wait_send()
        for i, k in enumerate(nearest_last(NZ)):
            z_copy(p, i, k).wait_send()
            z2_copy(p, i, k).wait_send()
        for i, k in enumerate(nearest_last(NY)):
            y_copy(p, i, k).wait_send()
        for i, (k, other) in enumerate(ENDS):
            f_copy(p, i, k, other).wait_send()
    in_store.wait()
    for c in kg_stores:
        c.wait()


def shards(scale, pre_act, out_grad, weights):
    to_rows = lambda t: jnp.swapaxes(t[0], 1, 2)
    vm, sem = pltpu.VMEM, pltpu.SemaphoreType.DMA
    grad, kernel_grad = pl.pallas_call(
        functools.partial(kernel, scale),
        out_shape=(
            jax.ShapeDtypeStruct((ROWS, C, W), BF16),
            jax.ShapeDtypeStruct((9 * BLK, 3 * W), F32),
        ),
        in_specs=[pl.BlockSpec(memory_space=pl.ANY)] * 3,
        out_specs=(pl.BlockSpec(memory_space=pl.ANY),) * 2,
        scratch_shapes=[
            vm((ROWS, C, W), BF16),
            vm((ROWS + 2, C, W), BF16),
            vm((3, 3, C, C), BF16),
            vm((ROWS, C, W), BF16),
            vm((3, 9 * BLK, W), F32),
            vm((C, ROWS * W), BF16),
            vm((LANES, (ROWS + 2) * W), BF16),
            vm((3, TILES, C, W), F32),
            vm((3, NX, C, W), F32),
            vm((3, NX, NZ, max(XROWS), W), BF16),
            vm((3, NX, NZ, max(XROWS), W), BF16),
            vm((3, NZ, NX, ZROWS - min(XROWS), W), BF16),
            vm((3, NZ, NX, ZROWS - min(XROWS), W), BF16),
            vm((3, NX, ZROWS - min(XROWS), W), F32),
            vm((3, NX, ZROWS - min(XROWS), W), F32),
            vm((3, NZ, max(XROWS), W), BF16),
            vm((3, NZ, max(XROWS), W), BF16),
            vm((3, NZ, max(XROWS), W), F32),
            vm((3, NY, ZROWS, W), BF16),
            vm((3, ZROWS, W), F32),
            vm((3, TILES, 24, W), F32),
            sem((3,)), sem((4,)), sem((2,)), sem((2,)), sem((3,)), sem((3,)),
            sem((3, 3)), sem((3, NX)), sem((3, 7)), sem((3, NZ)),
            sem((3, 3)), sem((3, NX)), sem((3, 7)), sem((3, NZ)),
            sem((3, 7)), sem((3, NY)), sem((3, 7)), sem((3, TILES)),
        ],
        compiler_params=pltpu.CompilerParams(collective_id=0, has_side_effects=True),
    )(to_rows(pre_act), to_rows(out_grad), weights)
    return jnp.swapaxes(grad, 1, 2)[None], kernel_grad[:, :C]


def solution(mesh):
    placed = P("dp", "space", None, None)

    def whole(pre_act, out_grad, weights):
        pixels = pre_act.shape[0] * pre_act.shape[1] * pre_act.shape[2]
        return jax.shard_map(
            functools.partial(shards, float(pixels) ** -0.5),
            mesh=mesh,
            in_specs=(placed, placed, P()),
            out_specs=(placed, P("dp", None)),
            check_vma=False,
        )(pre_act, out_grad, weights)

    return whole
```

time: 482 us -> 49.6 us (0.10)
  waiting for transfers between devices: 250 us -> 0 us
  blocking collectives: 105 us -> 0 us
  local copies, waits for them, and re-layouts: 82.7 us -> 3.66 us
  Pallas kernels: 0 us -> 45 us
  between operations: 14.9 us -> 0.64 us
  starting transfers between devices: 12.1 us -> 0 us
  matrix products: 9.18 us -> 0 us
  other arithmetic: 5.82 us -> 0 us
    psum x1 -> x0, waiting for transfers between devices: 250 us -> none  [shards(): summed = lax.psum(local_term, 'space')]
    unnamed x1 -> x0, blocking collectives: 105 us -> none
    pallas_call x0 -> x1, Pallas kernels: none -> 45 us  [shards(): pl.pallas_call(functools.partial(kernel, scale), out_shape=(jax.ShapeDtyp...]
    slice x10 -> x0, local copies, waits for them, and re-layouts: 26.7 us -> none  [shards(): grad_pad[:, 2 - tap_a:2 - tap_a + rows, 2 - tap_b:2 - tap_b + width, :]]
    another operation x11 -> x0, local copies, waits for them, and re-layouts: 20.5 us -> none  [the longest x10 20.1 us: shards(): grad_cols = jnp.stack(grad_taps, axis=3).reshape(count_rows, 9, chans)]
    unnamed x37 -> x2, local copies, waits for them, and re-layouts: 21.6 us -> 3.66 us
    mul x2 -> x0, local copies, waits for them, and re-layouts: 12.6 us -> none  [shards(): local_term = term.reshape(span * 9, chans) * factor]
    ppermute x2 -> x0, starting transfers between devices: 10.1 us -> none  [the longest x1 5.49 us: with_halo(): lax.ppermute(head, axis, [((i + 1) % count, i) for i in range(ends)])]
  transfers between devices with their start and end apart: 4 -> 0, of which waited for: 1 -> 0; matrix products, arithmetic and copies ran while one was open for 14% -> 0% of each run, Pallas kernels for 0% -> 0%
where the time goes in v2:
time: 49.6 us; the launch traced here: 49.3 us
  Pallas kernels  45 us (91%)
  local copies, waits for them, and re-layouts  3.66 us (7%)
  between operations  0.64 us (1%)
    pallas_call x1, Pallas kernels, shards(): pl.pallas_call(functools.partial(kernel, scale), out_shape=(jax.ShapeDtyp...  45 us
    unnamed x2, local copies, waits for them, and re-layouts  3.66 us

profile of v2, /device:TPU:1, one launch (start us, length us, event | category | flops | bytes accessed | tf_op | source)
XLA Modules:
  0.0 49.3 jit_solution(4490116749318694003)
XLA Ops:
  0.6 45.0 %shard_map.50 = (bf16[8,320,128]{2,1,0:T(8,128)(2,1)}, f32[180,384]{1,0:T(8,128)}) custom-call(bf16[8,320,128]{2,1,0:T(8,128)(2,1)} %bitcast.10, bf16[8,320,128]{2,1,0:T(8,128)(2,1)} %bitcast.11, bf16[3,3,320,320]{3,2,1,0:T(8,128)(2,1)} %k_hbm.1), custom_call_target="tpu_custom_call" | custom-call | tf_op jit(solution)/shard_map/pallas_call | solution.py:340
  45.7 2.0 %copy.7 = bf16[1,8,128,320]{2,3,1,0:T(8,128)(2,1)} copy(bf16[1,8,128,320]{2,3,1,0:T(8,128)(2,1)} %bitcast.12) | data formatting | bytes 1310720
  47.7 1.7 %copy.8 = f32[180,320]{1,0:T(8,128)} copy(f32[180,320]{1,0:T(8,128)} %bitcast.13) | data formatting | bytes 460800

commit v3 on v2

--- a/solution.py
+++ b/solution.py
@@ -90,12 +90,24 @@
         og2[pl.ds(0, C), lanes] = jnp.where(col == W - 1, 0.0, pltpu.roll(wide, W - 1, 1)).astype(BF16)
         og2[pl.ds(2 * C, C), lanes] = jnp.where(col == 0, 0.0, pltpu.roll(wide, 1, 1)).astype(BF16)
 
+    def product(act_lanes, og_lanes):
+        return lax.dot_general(
+            act2[:, act_lanes], og2[:, og_lanes], (((1,), (1,)), ((), ())), preferred_element_type=F32)
+
     def tap_row(p):
         a = PARTS[p]
-        total = lax.dot_general(
-            act2[...], og2[:, pl.ds((2 - a) * W, ROWS * W)], (((1,), (1,)), ((), ())), preferred_element_type=F32)
+        first = 1 if a == 2 else 0
+        count = ROWS if a == 1 else ROWS - 1
+        total = product(pl.ds(first * W, count * W), pl.ds((first + 2 - a) * W, count * W))
         for t in range(TILES):
             part_sum[p, t] = total[:, t * W : (t + 1) * W]
+
+    def edge_row(p):
+        a = PARTS[p]
+        row = 0 if a == 2 else ROWS - 1
+        total = product(pl.ds(row * W, W), pl.ds((row + 2 - a) * W, W))
+        for t in range(TILES):
+            part_sum[p, t] += total[:, t * W : (t + 1) * W]
 
     def core_copy(p):
         return pltpu.make_async_remote_copy(
@@ -281,14 +293,16 @@
     for c in halos:
         c.start()
     core_send(0)
+    tap_row(1)
     first_send(0)
+    tap_row(2)
     for i, (c, edge) in enumerate(zip(halos, (sp == 0, sp == 31))):
         c.wait_recv()
         r = i * (ROWS + 1)
         shifts(r, jnp.where(edge, jnp.zeros((C, W), BF16), og_v[r]))
-    tap_row(1)
+    edge_row(1)
     core_send(1)
-    tap_row(2)
+    edge_row(2)
     core_send(2)
     first_send(1)
     first_send(2)

time: 49.6 us -> 49.1 us (0.990)
  no operation moved by 1% of the time
where the time goes in v3:
time: 49.1 us; the launch traced here: 48.9 us
  Pallas kernels  44.6 us (91%)
  local copies, waits for them, and re-layouts  3.66 us (7%)
  between operations  0.64 us (1%)
    pallas_call x1, Pallas kernels, shards(): pl.pallas_call(functools.partial(kernel, scale), out_shape=(jax.ShapeDtyp...  44.6 us
    unnamed x2, local copies, waits for them, and re-layouts  3.66 us

profile of v3, /device:TPU:1, one launch (start us, length us, event | category | flops | bytes accessed | tf_op | source)
XLA Modules:
  0.0 48.9 jit_solution(2157049640355119014)
XLA Ops:
  0.6 44.6 %shard_map.50 = (bf16[8,320,128]{2,1,0:T(8,128)(2,1)}, f32[180,384]{1,0:T(8,128)}) custom-call(bf16[8,320,128]{2,1,0:T(8,128)(2,1)} %bitcast.10, bf16[8,320,128]{2,1,0:T(8,128)(2,1)} %bitcast.11, bf16[3,3,320,320]{3,2,1,0:T(8,128)(2,1)} %k_hbm.1), custom_call_target="tpu_custom_call" | custom-call | tf_op jit(solution)/shard_map/pallas_call | solution.py:354
  45.3 2.0 %copy.7 = bf16[1,8,128,320]{2,3,1,0:T(8,128)(2,1)} copy(bf16[1,8,128,320]{2,3,1,0:T(8,128)(2,1)} %bitcast.12) | data formatting | bytes 1310720
  47.2 1.7 %copy.8 = f32[180,320]{1,0:T(8,128)} copy(f32[180,320]{1,0:T(8,128)} %bitcast.13) | data formatting | bytes 460800
